TPU v7x, 32 devices: a whole 2x2x4 slice. The times are simulated.
32 devices in a mesh: blk: 16 (over z, x, core), feat: 2 (over y).
Axes of the slice: x: 2, y: 2, z: 4, core: 2. Of those that a mesh axis runs over, the one named last changes fastest.
Arguments:
- inputs: bfloat16 [4096, 1024], P('blk'), may hold values from -6 to 6
- col_mask: int32 [2, 1024], replicated, may hold values 0 or 1
- row_mask: int32 [4096], P('blk'), may hold values from 0 to 1
- width_class: int32 [4096], P('blk'), may hold values from 0 to 1
- frequencies: bfloat16 [2048, 2048], P(None, 'feat'), may hold values from -0.375 to 0.375
- phases: float32 [2048], P('feat'), may hold values from -3.140625 to 3.140625
- targets: float32 [4096], P('blk'), may hold values from -6 to 6
- prior_draws: float32 [4096, 16], P('blk'), may hold values from -6 to 6
- hidden_weight: float32 [1024, 2048], P('blk', 'feat'), may hold values from -0.1875 to 0.1875
- hidden_moment: float32 [1024, 2048], P('blk', 'feat'), may hold values from -9.536743e-06 to 9.536743e-06
- hidden_second: float32 [1024, 2048], P('blk', 'feat'), may hold values from 4.2e-14 to 1.7e-13
- alpha_weight: float32 [4096, 16], P('blk'), may hold values from -1.5 to 1.5
- alpha_moment: float32 [4096, 16], P('blk'), may hold values from -2.2888184e-05 to 2.2888184e-05
- alpha_second: float32 [4096, 16], P('blk'), may hold values from 1.7578125e-13 to 7.080078e-13
Outputs:
- norm_before: float32 [], replicated
- resid_norm: float32 [], replicated
- hidden_out: float32 [1024, 2048], P('blk', 'feat')
- hidden_moment_out: float32 [1024, 2048], P('blk', 'feat')
- hidden_second_out: float32 [1024, 2048], P('blk', 'feat')
- hidden_copy: bfloat16 [1024, 2048], P('blk', 'feat')
- alpha_out: float32 [4096, 16], P('blk')
- alpha_moment_out: float32 [4096, 16], P('blk')
- alpha_second_out: float32 [4096, 16], P('blk')
- alpha_copy: bfloat16 [4096, 16], P('blk')
All inputs are finite; a program needn't handle non-finite values.
Results may differ from a plain program's by a relative error of at most 0.0034.
Values may be sent and summed in bfloat16 or wider, within the bound.
No kernel may reach another device: no remote copies, remote signals or barrier semaphores. Data moves between devices by JAX's collectives and lax.ppermute only.
A program may use at most 192 MiB of HBM per device.

v0:
```python
import jax
import jax.numpy as jnp
from jax import lax
from jax.sharding import PartitionSpec as P

F = 2048
S = 16
ADAM_STEP = 10
PRECISE = lax.Precision.HIGHEST
NOISE = 0.01
CLIP_AT = 0.01
BETA_ONE = 0.9
BETA_TWO = 0.999
ADAM_EPS = 1e-08
DECAY = 0.01


def adamw_update(weight, moment, second, gradient, step_rate):
    moment = BETA_ONE * moment + (1.0 - BETA_ONE) * gradient
    second = BETA_TWO * second + (1.0 - BETA_TWO) * gradient * gradient
    moment_hat = moment / (1.0 - BETA_ONE**ADAM_STEP)
    second_hat = second / (1.0 - BETA_TWO**ADAM_STEP)
    weight = weight - step_rate * (moment_hat / (jnp.sqrt(second_hat) + ADAM_EPS) + DECAY * weight)
    return (weight, moment, second)


def kernel_step(features, pieces):
    kernel = jnp.einsum("tf,pf->tp", features, pieces[0], preferred_element_type=jnp.float32)
    fitted = jnp.dot(kernel, pieces[1].astype(jnp.float32), precision=PRECISE)
    summed = jnp.einsum("pf,ps->fs", pieces[0], pieces[1], preferred_element_type=jnp.float32)
    return (fitted, summed)


def on_device(
    inputs,
    col_mask,
    row_mask,
    width_class,
    frequencies,
    phases,
    targets,
    prior_draws,
    hidden_weight,
    hidden_moment,
    hidden_second,
    alpha_weight,
    alpha_moment,
    alpha_second,
):
    classes = col_mask.shape[0]
    feat_scale = (2.0 / F) ** 0.5
    onehot = (width_class[:, None] == jnp.arange(classes, dtype=jnp.int32)[None, :]).astype(
        jnp.float32
    )
    keep_cols = jnp.dot(onehot, col_mask.astype(jnp.float32))
    masked = inputs * keep_cols.astype(jnp.bfloat16)
    keep_rows = row_mask.astype(jnp.float32)
    true_count = jnp.maximum(lax.psum(jnp.sum(keep_rows), "blk"), 1.0)
    columns = masked
    first_pre = jnp.dot(
        columns,
        lax.all_gather(hidden_weight.astype(jnp.bfloat16), "blk", axis=0, tiled=True),
        preferred_element_type=jnp.float32,
    )
    tanh_full = jnp.tanh(first_pre)
    hidden = tanh_full.astype(jnp.bfloat16)
    pre = jnp.dot(
        lax.all_gather(hidden, "feat", axis=1, tiled=True),
        frequencies,
        preferred_element_type=jnp.float32,
    )
    phase_arg = pre + phases[None, :]
    features = (feat_scale * jnp.cos(phase_arg)).astype(jnp.bfloat16)
    alpha_low = alpha_weight.astype(jnp.bfloat16)

    def fold_step(pieces):
        return kernel_step(features, pieces)

    fitted_part, moments = fold_step(
        (
            lax.all_gather(features, "blk", axis=0, tiled=True),
            lax.all_gather(alpha_low, "blk", axis=0, tiled=True),
        )
    )
    fitted = lax.psum(fitted_part, "feat") + NOISE * alpha_weight
    residual = fitted - targets[:, None] - prior_draws
    resid_grad = (2.0 * keep_rows[:, None] * residual / (true_count * S)).astype(jnp.bfloat16)
    pulled_part, back_moments = fold_step(
        (
            lax.all_gather(features, "blk", axis=0, tiled=True),
            lax.all_gather(resid_grad, "blk", axis=0, tiled=True),
        )
    )
    alpha_grad = lax.psum(pulled_part, "feat") + NOISE * resid_grad.astype(jnp.float32)
    feature_grad = jnp.dot(resid_grad.astype(jnp.float32), moments.T, precision=PRECISE)
    feature_grad = feature_grad + jnp.dot(
        alpha_low.astype(jnp.float32), back_moments.T, precision=PRECISE
    )
    pre_grad = (-feat_scale * jnp.sin(phase_arg) * feature_grad).astype(jnp.bfloat16)
    hidden_terms = jnp.einsum(
        "tf,hf->th", pre_grad, frequencies, preferred_element_type=jnp.float32
    )
    hidden_grad = lax.psum_scatter(hidden_terms, "feat", scatter_dimension=1, tiled=True)
    first_grad = ((1.0 - tanh_full * tanh_full) * hidden_grad).astype(jnp.bfloat16)
    columns = masked
    weight_grad = lax.psum_scatter(
        jnp.einsum("td,th->dh", columns, first_grad, preferred_element_type=jnp.float32),
        "blk",
        scatter_dimension=0,
        tiled=True,
    )
    first_feat = (lax.axis_index("feat") == 0).astype(jnp.float32)
    grad_part = jnp.sum(weight_grad * weight_grad) + first_feat * jnp.sum(alpha_grad * alpha_grad)
    resid_part = first_feat * jnp.sum(keep_rows[:, None] * residual * residual)
    grad_total, resid_total = lax.psum((grad_part, resid_part), ("blk", "feat"))
    norm_before = jnp.sqrt(grad_total)
    resid_norm = jnp.sqrt(resid_total)
    clip = jnp.minimum(1.0, CLIP_AT / (norm_before + 1e-06))
    hidden_out, moment_out, second_out = adamw_update(
        hidden_weight, hidden_moment, hidden_second, weight_grad * clip, 0.02
    )
    alpha_out, alpha_moment_out, alpha_second_out = adamw_update(
        alpha_weight, alpha_moment, alpha_second, alpha_grad * clip, 0.05
    )
    return (
        norm_before,
        resid_norm,
        hidden_out,
        moment_out,
        second_out,
        hidden_out.astype(jnp.bfloat16),
        alpha_out,
        alpha_moment_out,
        alpha_second_out,
        alpha_out.astype(jnp.bfloat16),
    )


def solution(mesh):
    in_specs = (
        P("blk", None),
        P(),
        P("blk"),
        P("blk"),
        P(None, "feat"),
        P("feat"),
        P("blk"),
        P("blk", None),
        P("blk", "feat"),
        P("blk", "feat"),
        P("blk", "feat"),
        P("blk", None),
        P("blk", None),
        P("blk", None),
    )
    out_specs = (
        P(),
        P(),
        P("blk", "feat"),
        P("blk", "feat"),
        P("blk", "feat"),
        P("blk", "feat"),
        P("blk", None),
        P("blk", None),
        P("blk", None),
        P("blk", None),
    )
    return jax.shard_map(
        on_device, mesh=mesh, in_specs=in_specs, out_specs=out_specs, check_vma=False
    )
```

profile of v0, /device:TPU:0, one launch (start us, length us, event | category | flops | bytes accessed | tf_op | source)
XLA Modules:
  0.0 378.5 jit_solution(18336091625798306020)
XLA Ops:
  7.2 0.0 copy-start.11
  7.2 0.0 all-gather.4.cloned.1.call-start
  7.2 1.6 convert_element_type.47
  8.9 0.0 all-gather.4.cloned.1.call-update
  8.9 0.0 all-gather.6.cloned.1.call-start
  8.9 1.4 fusion.3
  10.3 44.6 %all-gather.4.cloned.1.call-done = bf16[1024,1024]{1,0:T(8,128)(2,1)} async-done(((bf16[64,1024]{1,0:T(8,128)(2,1)}), bf16[1024,1024]{1,0:T(8,128)(2,1)}) %all-gather.4.cloned.1.call-update) | async-done | bytes 2097168 | tf_op jit(solution)/shard_map/all_gather | solution.py:62
  54.9 3.1 fusion.16
  58.1 0.0 all-gather.6.cloned.1.call-update
  58.1 0.0 copy-start.8
  58.1 0.0 copy-start.4
  58.1 0.0 all-gather.8.cloned.1.call-start
  58.2 20.1 %all-gather.6.cloned.1.call-done = bf16[256,2048]{1,0:T(8,128)(2,1)} async-done(((bf16[256,1024]{1,0:T(8,128)(2,1)}), bf16[256,2048]{1,0:T(8,128)(2,1)}) %all-gather.6.cloned.1.call-update) | async-done | bytes 1048592 | tf_op jit(solution)/shard_map/all_gather | solution.py:68
  78.3 0.0 copy-done.11
  78.3 7.3 %multiply_convert_fusion.1 = (bf16[256,1024]{1,0:T(8,128)(2,1)}, f32[256,1024]{1,0:T(8,128)S(1)}) fusion(f32[1024]{0:T(1024)S(1)} %copy-done.11, bf16[256,2048]{1,0:T(8,128)(2,1)} %all-gather.6.cloned.1.call-done, bf16[2048,1024]{1,0:T(8,128)(2,1)} %param.18), kind=kOutput, calls=%fused_computation.9 | convolution fusion | flops 1074528256 | bytes 6819840 | tf_op jit(solution)/shard_map/dot_general | solution.py:67
  85.6 0.0 all-gather.8.cloned.1.call-update
  85.6 0.0 reduce-scatter.3.cloned.1.call-start
  85.6 0.0 copy-done.8
  85.6 0.6 broadcast_multiply_fusion
  86.2 34.6 %psum.36 = f32[]{:T(128)} all-reduce(f32[]{:T(128)} %get-tuple-element.23), channel_id=1, replica_groups=mesh['blk'=16,'feat'=2] {'blk'}, use_global_device_ids=true, to_apply=%region_2.0 | all-reduce | flops 1 | bytes 8 | tf_op jit(solution)/shard_map/psum | solution.py:58
  121.5 18.8 %all_gather.19 = bf16[4096,16]{0,1:T(8,128)(2,1)S(1)} all-gather(bf16[256,16]{0,1:T(8,128)(2,1)S(1)} %convert_element_type.51), channel_id=1, replica_groups=mesh['blk'=16,'feat'=2] {'blk'}, dimensions={0}, use_global_device_ids=true | all-gather | bytes 139264 | tf_op jit(solution)/shard_map/all_gather | solution.py:82
  140.2 20.7 %all-gather.8.cloned.1.call-done = bf16[4096,1024]{1,0:T(8,128)(2,1)} async-done(((bf16[256,1024]{1,0:T(8,128)(2,1)}), bf16[4096,1024]{1,0:T(8,128)(2,1)}) %all-gather.8.cloned.1.call-update) | async-done | bytes 8388624 | tf_op jit(solution)/shard_map/all_gather | solution.py:81
  160.9 5.9 %fusion.17 = f32[256,4096]{1,0:T(8,128)S(1)} fusion(bf16[256,1024]{1,0:T(8,128)(2,1)} %get-tuple-element.26, bf16[4096,1024]{1,0:T(8,128)(2,1)} %all-gather.8.cloned.1.call-done), kind=kOutput, calls=%fused_computation.36 | convolution fusion | flops 2147483648 | bytes 13107200 | tf_op jit(solution)/shard_map/tf,pf->tp/dot_general | solution.py:28
  166.9 1.9 copy-done
  168.8 2.0 fusion.18
  170.8 8.3 %psum.35 = f32[256,16]{0,1:T(8,128)S(1)} all-reduce(f32[256,16]{0,1:T(8,128)S(1)} %fusion.18), channel_id=1, replica_groups=mesh['blk'=16,'feat'=2] {'feat'}, use_global_device_ids=true, to_apply=%region_0.0 | all-reduce | flops 4096 | bytes 32768 | tf_op jit(solution)/shard_map/psum | solution.py:85
  179.2 0.6 fusion.8
  179.8 19.3 %all_gather.20 = bf16[4096,16]{0,1:T(8,128)(2,1)S(1)} all-gather(bf16[256,16]{0,1:T(8,128)(2,1)S(1)} %divide_convert_fusion), channel_id=1, replica_groups=mesh['blk'=16,'feat'=2] {'blk'}, dimensions={0}, use_global_device_ids=true | all-gather | bytes 139264 | tf_op jit(solution)/shard_map/all_gather | solution.py:91
  199.1 5.8 %fusion.19 = f32[1024,16]{1,0:T(8,128)S(1)} fusion(bf16[4096,1024]{1,0:T(8,128)(2,1)} %all-gather.8.cloned.1.call-done, bf16[4096,16]{0,1:T(8,128)(2,1)S(1)} %all_gather.19), kind=kOutput, calls=%fused_computation.38 | convolution fusion | flops 134217728 | bytes 8585216 | tf_op jit(solution)/shard_map/pf,ps->fs/dot_general | solution.py:30
  204.8 0.6 fusion.20
  205.5 0.0 copy-start.10
  205.5 5.9 %fusion.21 = f32[1024,16]{1,0:T(8,128)S(1)} fusion(bf16[4096,1024]{1,0:T(8,128)(2,1)} %all-gather.8.cloned.1.call-done, bf16[4096,16]{0,1:T(8,128)(2,1)S(1)} %all_gather.20), kind=kOutput, calls=%fused_computation.40 | convolution fusion | flops 134217728 | bytes 8585216 | tf_op jit(solution)/shard_map/pf,ps->fs/dot_general | solution.py:30
  211.4 4.3 %fusion.2 = bf16[256,1024]{1,0:T(8,128)(2,1)S(1)} fusion(f32[256,1024]{1,0:T(8,128)S(1)} %fusion.20, f32[1024,16]{1,0:T(8,128)S(1)} %fusion.21, bf16[256,16]{0,1:T(8,128)(2,1)S(1)} %convert_element_type.51, f32[256,1024]{1,0:T(8,128)S(1)} %get-tuple-element.27), kind=kOutput, calls=%fused_computation.5 | convolution fusion | flops 51380224 | bytes 2695168 | tf_op jit(solution)/shard_map/dot_general | solution.py:96
  215.7 2.6 fusion.22
  218.3 0.0 reduce-scatter.3.cloned.1.call-update
  218.3 0.0 reduce-scatter.5.cloned.1.call-start
  218.4 28.4 %reduce-scatter.3.cloned.1.call-done = f32[256,1024]{1,0:T(8,128)} async-done(((f32[256,2048]{1,0:T(8,128)}), f32[256,1024]{1,0:T(8,128)}) %reduce-scatter.3.cloned.1.call-update) | async-done | bytes 1048592 | tf_op jit(solution)/shard_map/reduce_scatter | solution.py:103
  246.8 3.9 %fusion.4 = f32[1024,1024]{1,0:T(8,128)} fusion(bf16[256,1024]{1,0:T(8,128)(2,1)S(1)} %fusion.3, f32[256,1024]{1,0:T(8,128)} %reduce-scatter.3.cloned.1.call-done, f32[256,1024]{1,0:T(8,128)S(1)} %get-tuple-element.25), kind=kOutput, calls=%fused_computation.10 | convolution fusion | flops 537919488 | bytes 6815744 | tf_op jit(solution)/shard_map/td,th->dh/dot_general | solution.py:107
  250.8 0.0 copy-start.3
  250.8 0.0 reduce-scatter.5.cloned.1.call-update
  251.5 4.2 %fusion.23 = f32[256,16]{0,1:T(8,128)S(1)} fusion(f32[256,4096]{1,0:T(8,128)} %copy-done, bf16[4096,16]{0,1:T(8,128)(2,1)S(1)} %all_gather.20), kind=kOutput, calls=%fused_computation.42 | convolution fusion | flops 201326592 | bytes 4341760 | tf_op jit(solution)/shard_map/dot_general | solution.py:29
  255.7 7.0 %psum.37 = f32[256,16]{0,1:T(8,128)S(1)} all-reduce(f32[256,16]{0,1:T(8,128)S(1)} %fusion.23), channel_id=1, replica_groups=mesh['blk'=16,'feat'=2] {'feat'}, use_global_device_ids=true, to_apply=%region_6.0 | all-reduce | flops 4096 | bytes 32768 | tf_op jit(solution)/shard_map/psum | solution.py:94
  262.7 0.6 multiply_reduce_fusion.1
  264.0 59.8 %reduce-scatter.5.cloned.1.call-done = f32[64,1024]{1,0:T(8,128)} async-done(((f32[1024,1024]{1,0:T(8,128)}), f32[64,1024]{1,0:T(8,128)}) %reduce-scatter.5.cloned.1.call-update) | async-done | bytes 262160 | tf_op jit(solution)/shard_map/reduce_scatter | solution.py:106
  323.7 1.6 multiply_reduce_fusion
  326.0 39.6 %all-reduce = (f32[]{:T(128)}, f32[]{:T(128)}) all-reduce(f32[]{:T(128)S(6)} %add.72, f32[]{:T(128)S(6)} %mul.177), channel_id=1, replica_groups=mesh['blk'=16,'feat'=2] {'blk','feat'}, use_global_device_ids=true, to_apply=%region_8.0 | all-reduce | flops 2 | bytes 16 | tf_op jit(solution)/shard_map/psum | solution.py:115
  367.0 0.6 fusion.12
  367.7 2.0 fusion.14
  (19 shorter events, 0.0 us)
Async XLA Ops:
  7.2 71.1 %copy-start.11 = (f32[1024]{0:T(1024)S(1)}, f32[1024]{0:T(1024)}, u32[]{:S(2)}) copy-start(f32[1024]{0:T(1024)} %param.19) | copy-start | bytes 12292
  7.2 47.8 %all-gather.4.cloned.1.call-start = ((), (), s32[]{:S(2)}) async-start(), calls=%async_computation.2 | async-start | bytes 2228224 | tf_op jit(solution)/shard_map/all_gather | solution.py:62
  8.9 69.4 %all-gather.6.cloned.1.call-start = ((), (), s32[]{:S(2)}) async-start(), calls=%async_computation.3 | async-start | bytes 1572864 | tf_op jit(solution)/shard_map/all_gather | solution.py:68
  58.1 27.5 %copy-start.8 = (s32[256]{0:T(256)S(1)}, s32[256]{0:T(256)}, u32[]{:S(2)}) copy-start(s32[256]{0:T(256)} %param.16) | copy-start | bytes 3076
  58.1 62.7 %copy-start.4 = (f32[256,16]{0,1:T(8,128)S(1)}, f32[256,16]{0,1:T(8,128)}, u32[]{:S(2)}) copy-start(f32[256,16]{0,1:T(8,128)} %param.25) | copy-start | bytes 49156
  58.1 102.8 %all-gather.8.cloned.1.call-start = ((), (), s32[]{:S(2)}) async-start(), calls=%async_computation.4 | async-start | bytes 8912896 | tf_op jit(solution)/shard_map/all_gather | solution.py:81
  85.6 161.2 %reduce-scatter.3.cloned.1.call-start = ((), (), s32[]{:S(2)}) async-start(), calls=%async_computation.5 | async-start | bytes 3145728 | tf_op jit(solution)/shard_map/reduce_scatter | solution.py:103
  166.9 1.9 copy-start
  168.8 10.3 %copy-start.7 = (f32[256,16]{0,1:T(8,128)S(1)}, f32[256,16]{0,1:T(8,128)}, u32[]{:S(2)}) copy-start(f32[256,16]{0,1:T(8,128)} %param.21) | copy-start | bytes 49156
  168.8 10.3 %copy-start.9 = (f32[256]{0:T(256)S(1)}, f32[256]{0:T(256)}, u32[]{:S(2)}) copy-start(f32[256]{0:T(256)} %param.20) | copy-start | bytes 3076
  205.5 10.2 %copy-start.10 = (bf16[2048,1024]{1,0:T(8,128)(2,1)S(1)}, bf16[2048,1024]{1,0:T(8,128)(2,1)}, u32[]{:S(2)}) copy-start(bf16[2048,1024]{1,0:T(8,128)(2,1)} %param.18) | copy-start | bytes 12582916
  218.3 105.4 %reduce-scatter.5.cloned.1.call-start = ((), (), s32[]{:S(2)}) async-start(), calls=%async_computation.6 | async-start | bytes 4456448 | tf_op jit(solution)/shard_map/reduce_scatter | solution.py:106
  250.8 116.3 %copy-start.5 = (f32[256,16]{0,1:T(8,128)S(1)}, f32[256,16]{0,1:T(8,128)}, u32[]{:S(2)}) copy-start(f32[256,16]{0,1:T(8,128)} %param.26) | copy-start | bytes 49156
  250.8 116.3 %copy-start.6 = (f32[256,16]{0,1:T(8,128)S(1)}, f32[256,16]{0,1:T(8,128)}, u32[]{:S(2)}) copy-start(f32[256,16]{0,1:T(8,128)} %param.27) | copy-start | bytes 49156
  250.8 116.9 %copy-start.1 = (f32[64,1024]{1,0:T(8,128)S(1)}, f32[64,1024]{1,0:T(8,128)}, u32[]{:S(2)}) copy-start(f32[64,1024]{1,0:T(8,128)} %param.22) | copy-start | bytes 786436
  250.8 116.9 %copy-start.2 = (f32[64,1024]{1,0:T(8,128)S(1)}, f32[64,1024]{1,0:T(8,128)}, u32[]{:S(2)}) copy-start(f32[64,1024]{1,0:T(8,128)} %param.23) | copy-start | bytes 786436
  250.8 116.9 %copy-start.3 = (f32[64,1024]{1,0:T(8,128)S(1)}, f32[64,1024]{1,0:T(8,128)}, u32[]{:S(2)}) copy-start(f32[64,1024]{1,0:T(8,128)} %param.24) | copy-start | bytes 786436
Sparse Core Ops, SparseCore 0:
  10.7 44.1 all-gather.3
  58.2 19.9 all-gather.5
  85.7 75.1 all-gather.7
  218.4 28.3 reduce-scatter.2
  250.9 72.7 reduce-scatter.4
where the time goes:
time: 379 us; the launch traced here: 378 us
  waiting for transfers between devices  174 us (46%)
  blocking collectives  128 us (34%)
  matrix products  47.1 us (12%)
  between operations  20.3 us (5%)
  other arithmetic  7.74 us (2%)
    reduce_scatter x1, waiting for transfers between devices, on_device(): lax.psum_scatter(jnp.einsum('td,th->dh', columns, first_grad, preferred_e...  59.8 us
    all_gather x1, waiting for transfers between devices, on_device(): lax.all_gather(hidden_weight.astype(jnp.bfloat16), 'blk', axis=0, tiled=T...  44.6 us
    psum x1, blocking collectives, on_device(): grad_total, resid_total = lax.psum((grad_part, resid_part), ('blk', 'feat'))  39.6 us
    psum x1, blocking collectives, on_device(): true_count = jnp.maximum(lax.psum(jnp.sum(keep_rows), 'blk'), 1.0)  34.6 us
    reduce_scatter x1, waiting for transfers between devices, on_device(): lax.psum_scatter(hidden_terms, 'feat', scatter_dimension=1, tiled=True)  28.4 us
    all_gather x1, waiting for transfers between devices, on_device(): lax.all_gather(features, 'blk', axis=0, tiled=True)  20.7 us
    all_gather x1, waiting for transfers between devices, on_device(): lax.all_gather(hidden, 'feat', axis=1, tiled=True)  20.1 us
    all_gather x1, blocking collectives, on_device(): lax.all_gather(resid_grad, 'blk', axis=0, tiled=True)  19.3 us
  transfers between devices with their start and end apart: 5, of which 5 were waited for; matrix products, arithmetic and copies ran while one was open for 2% of the time, Pallas kernels for 0%

commit v1 on v0

--- a/solution.py
+++ b/solution.py
@@ -82,7 +82,7 @@
             lax.all_gather(alpha_low, "blk", axis=0, tiled=True),
         )
     )
-    fitted = lax.psum(fitted_part, "feat") + NOISE * alpha_weight
+    fitted = jnp.sum(lax.all_gather(fitted_part, "feat"), 0) + NOISE * alpha_weight
     residual = fitted - targets[:, None] - prior_draws
     resid_grad = (2.0 * keep_rows[:, None] * residual / (true_count * S)).astype(jnp.bfloat16)
     pulled_part, back_moments = fold_step(

time: 379 us -> 376 us (level)
  blocking collectives: 128 us -> 124 us
    psum x1 -> x0, blocking collectives: 8.33 us -> none  [on_device(): fitted = lax.psum(fitted_part, 'feat') + NOISE * alpha_weight]
    all_gather x0 -> x1, blocking collectives: none -> 4.42 us  [on_device(): lax.all_gather(fitted_part, 'feat')]
where the time goes in v1:
time: 376 us
  waiting for transfers between devices  174 us (46%)
  blocking collectives  124 us (33%)
  matrix products  47.1 us (13%)
  between operations  20.3 us (5%)
  other arithmetic  7.78 us (2%)
    reduce_scatter x1, waiting for transfers between devices, on_device(): lax.psum_scatter(jnp.einsum('td,th->dh', columns, first_grad, preferred_e...  59.8 us
    all_gather x1, waiting for transfers between devices, on_device(): lax.all_gather(hidden_weight.astype(jnp.bfloat16), 'blk', axis=0, tiled=T...  44.6 us
    psum x1, blocking collectives, on_device(): grad_total, resid_total = lax.psum((grad_part, resid_part), ('blk', 'feat'))  39.5 us
    psum x1, blocking collectives, on_device(): true_count = jnp.maximum(lax.psum(jnp.sum(keep_rows), 'blk'), 1.0)  34.6 us
    reduce_scatter x1, waiting for transfers between devices, on_device(): lax.psum_scatter(hidden_terms, 'feat', scatter_dimension=1, tiled=True)  29.1 us
    all_gather x1, waiting for transfers between devices, on_device(): lax.all_gather(features, 'blk', axis=0, tiled=True)  20.7 us
    all_gather x1, waiting for transfers between devices, on_device(): lax.all_gather(hidden, 'feat', axis=1, tiled=True)  20.1 us
    all_gather x1, blocking collectives, on_device(): lax.all_gather(resid_grad, 'blk', axis=0, tiled=True)  19.6 us
  transfers between devices with their start and end apart: 5, of which 5 were waited for; matrix products, arithmetic and copies ran while one was open for 2% of the time, Pallas kernels for 0%

profile of v1, /device:TPU:0, one launch (start us, length us, event | category | flops | bytes accessed | tf_op | source)
XLA Modules:
  0.0 375.7 jit_solution(3853858654798396619)
XLA Ops:
  7.2 0.0 copy-start.11
  7.2 0.0 all-gather.5.cloned.1.call-start
  7.2 1.6 convert_element_type.47
  8.9 0.0 all-gather.5.cloned.1.call-update
  8.9 0.0 all-gather.7.cloned.1.call-start
  8.9 1.4 fusion.3
  10.3 44.6 %all-gather.5.cloned.1.call-done = bf16[1024,1024]{1,0:T(8,128)(2,1)} async-done(((bf16[64,1024]{1,0:T(8,128)(2,1)}), bf16[1024,1024]{1,0:T(8,128)(2,1)}) %all-gather.5.cloned.1.call-update) | async-done | bytes 2097168 | tf_op jit(solution)/shard_map/all_gather | solution.py:62
  54.9 3.1 fusion.16
  58.1 0.0 all-gather.7.cloned.1.call-update
  58.1 0.0 copy-start.8
  58.1 0.0 copy-start.4
  58.1 0.0 all-gather.9.cloned.1.call-start
  58.2 20.1 %all-gather.7.cloned.1.call-done = bf16[256,2048]{1,0:T(8,128)(2,1)} async-done(((bf16[256,1024]{1,0:T(8,128)(2,1)}), bf16[256,2048]{1,0:T(8,128)(2,1)}) %all-gather.7.cloned.1.call-update) | async-done | bytes 1048592 | tf_op jit(solution)/shard_map/all_gather | solution.py:68
  78.3 0.0 copy-done.11
  78.3 7.3 %multiply_convert_fusion.1 = (bf16[256,1024]{1,0:T(8,128)(2,1)}, f32[256,1024]{1,0:T(8,128)S(1)}) fusion(f32[1024]{0:T(1024)S(1)} %copy-done.11, bf16[256,2048]{1,0:T(8,128)(2,1)} %all-gather.7.cloned.1.call-done, bf16[2048,1024]{1,0:T(8,128)(2,1)} %param.18), kind=kOutput, calls=%fused_computation.9 | convolution fusion | flops 1074528256 | bytes 6819840 | tf_op jit(solution)/shard_map/dot_general | solution.py:67
  85.6 0.0 all-gather.9.cloned.1.call-update
  85.6 0.0 reduce-scatter.3.cloned.1.call-start
  85.6 0.6 broadcast_multiply_fusion
  86.2 34.6 %psum.28 = f32[]{:T(128)} all-reduce(f32[]{:T(128)} %get-tuple-element.23), channel_id=1, replica_groups=mesh['blk'=16,'feat'=2] {'blk'}, use_global_device_ids=true, to_apply=%region_2.0 | all-reduce | flops 1 | bytes 8 | tf_op jit(solution)/shard_map/psum | solution.py:58
  121.5 18.8 %all_gather.25 = bf16[4096,16]{0,1:T(8,128)(2,1)S(1)} all-gather(bf16[256,16]{0,1:T(8,128)(2,1)S(1)} %convert_element_type.51), channel_id=1, replica_groups=mesh['blk'=16,'feat'=2] {'blk'}, dimensions={0}, use_global_device_ids=true | all-gather | bytes 139264 | tf_op jit(solution)/shard_map/all_gather | solution.py:82
  140.2 20.7 %all-gather.9.cloned.1.call-done = bf16[4096,1024]{1,0:T(8,128)(2,1)} async-done(((bf16[256,1024]{1,0:T(8,128)(2,1)}), bf16[4096,1024]{1,0:T(8,128)(2,1)}) %all-gather.9.cloned.1.call-update) | async-done | bytes 8388624 | tf_op jit(solution)/shard_map/all_gather | solution.py:81
  160.9 5.9 %fusion.17 = f32[256,4096]{1,0:T(8,128)S(1)} fusion(bf16[256,1024]{1,0:T(8,128)(2,1)} %get-tuple-element.26, bf16[4096,1024]{1,0:T(8,128)(2,1)} %all-gather.9.cloned.1.call-done), kind=kOutput, calls=%fused_computation.36 | convolution fusion | flops 2147483648 | bytes 13107200 | tf_op jit(solution)/shard_map/tf,pf->tp/dot_general | solution.py:28
  166.9 1.9 copy-done
  168.8 2.0 fusion.18
  170.8 4.4 %all-gather = f32[512,16]{0,1:T(8,128)S(1)} all-gather(f32[256,16]{0,1:T(8,128)S(1)} %fusion.18), channel_id=2, replica_groups=mesh['blk'=16,'feat'=2] {'feat'}, dimensions={0}, use_global_device_ids=true | all-gather | bytes 49152 | tf_op jit(solution)/shard_map/all_gather | solution.py:85
  175.3 0.6 fusion.8
  176.0 19.6 %all_gather.28 = bf16[4096,16]{0,1:T(8,128)(2,1)S(1)} all-gather(bf16[256,16]{0,1:T(8,128)(2,1)S(1)} %divide_convert_fusion), channel_id=1, replica_groups=mesh['blk'=16,'feat'=2] {'blk'}, dimensions={0}, use_global_device_ids=true | all-gather | bytes 139264 | tf_op jit(solution)/shard_map/all_gather | solution.py:91
  195.6 5.8 %fusion.19 = f32[1024,16]{1,0:T(8,128)S(1)} fusion(bf16[4096,1024]{1,0:T(8,128)(2,1)} %all-gather.9.cloned.1.call-done, bf16[4096,16]{0,1:T(8,128)(2,1)S(1)} %all_gather.25), kind=kOutput, calls=%fused_computation.38 | convolution fusion | flops 134217728 | bytes 8585216 | tf_op jit(solution)/shard_map/pf,ps->fs/dot_general | solution.py:30
  201.3 0.6 fusion.20
  201.9 0.0 copy-start.10
  202.0 5.9 %fusion.21 = f32[1024,16]{1,0:T(8,128)S(1)} fusion(bf16[4096,1024]{1,0:T(8,128)(2,1)} %all-gather.9.cloned.1.call-done, bf16[4096,16]{0,1:T(8,128)(2,1)S(1)} %all_gather.28), kind=kOutput, calls=%fused_computation.40 | convolution fusion | flops 134217728 | bytes 8585216 | tf_op jit(solution)/shard_map/pf,ps->fs/dot_general | solution.py:30
  207.9 4.3 %fusion.2 = bf16[256,1024]{1,0:T(8,128)(2,1)S(1)} fusion(f32[256,1024]{1,0:T(8,128)S(1)} %fusion.20, f32[1024,16]{1,0:T(8,128)S(1)} %fusion.21, bf16[256,16]{0,1:T(8,128)(2,1)S(1)} %convert_element_type.51, f32[256,1024]{1,0:T(8,128)S(1)} %get-tuple-element.27), kind=kOutput, calls=%fused_computation.5 | convolution fusion | flops 51380224 | bytes 2695168 | tf_op jit(solution)/shard_map/dot_general | solution.py:96
  212.2 2.6 fusion.22
  214.8 0.0 reduce-scatter.3.cloned.1.call-update
  214.8 0.0 reduce-scatter.5.cloned.1.call-start
  214.9 29.1 %reduce-scatter.3.cloned.1.call-done = f32[256,1024]{1,0:T(8,128)} async-done(((f32[256,2048]{1,0:T(8,128)}), f32[256,1024]{1,0:T(8,128)}) %reduce-scatter.3.cloned.1.call-update) | async-done | bytes 1048592 | tf_op jit(solution)/shard_map/reduce_scatter | solution.py:103
  244.0 3.9 %fusion.4 = f32[1024,1024]{1,0:T(8,128)} fusion(bf16[256,1024]{1,0:T(8,128)(2,1)S(1)} %fusion.3, f32[256,1024]{1,0:T(8,128)} %reduce-scatter.3.cloned.1.call-done, f32[256,1024]{1,0:T(8,128)S(1)} %get-tuple-element.25), kind=kOutput, calls=%fused_computation.10 | convolution fusion | flops 537919488 | bytes 6815744 | tf_op jit(solution)/shard_map/td,th->dh/dot_general | solution.py:107
  247.9 0.0 copy-start.3
  247.9 0.0 reduce-scatter.5.cloned.1.call-update
  248.7 4.2 %fusion.23 = f32[256,16]{0,1:T(8,128)S(1)} fusion(f32[256,4096]{1,0:T(8,128)} %copy-done, bf16[4096,16]{0,1:T(8,128)(2,1)S(1)} %all_gather.28), kind=kOutput, calls=%fused_computation.42 | convolution fusion | flops 201326592 | bytes 4341760 | tf_op jit(solution)/shard_map/dot_general | solution.py:29
  252.9 7.0 %psum.29 = f32[256,16]{0,1:T(8,128)S(1)} all-reduce(f32[256,16]{0,1:T(8,128)S(1)} %fusion.23), channel_id=1, replica_groups=mesh['blk'=16,'feat'=2] {'feat'}, use_global_device_ids=true, to_apply=%region_6.0 | all-reduce | flops 4096 | bytes 32768 | tf_op jit(solution)/shard_map/psum | solution.py:94
  259.9 0.6 multiply_reduce_fusion.1
  261.1 59.8 %reduce-scatter.5.cloned.1.call-done = f32[64,1024]{1,0:T(8,128)} async-done(((f32[1024,1024]{1,0:T(8,128)}), f32[64,1024]{1,0:T(8,128)}) %reduce-scatter.5.cloned.1.call-update) | async-done | bytes 262160 | tf_op jit(solution)/shard_map/reduce_scatter | solution.py:106
  321.0 1.6 multiply_reduce_fusion
  323.3 39.5 %all-reduce = (f32[]{:T(128)}, f32[]{:T(128)}) all-reduce(f32[]{:T(128)S(6)} %add.70, f32[]{:T(128)S(6)} %mul.177), channel_id=1, replica_groups=mesh['blk'=16,'feat'=2] {'blk','feat'}, use_global_device_ids=true, to_apply=%region_8.0 | all-reduce | flops 2 | bytes 16 | tf_op jit(solution)/shard_map/psum | solution.py:115
  364.2 0.6 fusion.12
  364.9 0.0 copy-done.3
  364.9 2.0 fusion.14
  (21 shorter events, 0.1 us)
Async XLA Ops:
  7.2 71.1 %copy-start.11 = (f32[1024]{0:T(1024)S(1)}, f32[1024]{0:T(1024)}, u32[]{:S(2)}) copy-start(f32[1024]{0:T(1024)} %param.19) | copy-start | bytes 12292
  7.2 47.8 %all-gather.5.cloned.1.call-start = ((), (), s32[]{:S(2)}) async-start(), calls=%async_computation.2 | async-start | bytes 2228224 | tf_op jit(solution)/shard_map/all_gather | solution.py:62
  8.9 69.4 %all-gather.7.cloned.1.call-start = ((), (), s32[]{:S(2)}) async-start(), calls=%async_computation.3 | async-start | bytes 1572864 | tf_op jit(solution)/shard_map/all_gather | solution.py:68
  58.1 27.5 %copy-start.8 = (s32[256]{0:T(256)S(1)}, s32[256]{0:T(256)}, u32[]{:S(2)}) copy-start(s32[256]{0:T(256)} %param.16) | copy-start | bytes 3076
  58.1 62.7 %copy-start.4 = (f32[256,16]{0,1:T(8,128)S(1)}, f32[256,16]{0,1:T(8,128)}, u32[]{:S(2)}) copy-start(f32[256,16]{0,1:T(8,128)} %param.25) | copy-start | bytes 49156
  58.1 102.8 %all-gather.9.cloned.1.call-start = ((), (), s32[]{:S(2)}) async-start(), calls=%async_computation.4 | async-start | bytes 8912896 | tf_op jit(solution)/shard_map/all_gather | solution.py:81
  85.6 158.4 %reduce-scatter.3.cloned.1.call-start = ((), (), s32[]{:S(2)}) async-start(), calls=%async_computation.5 | async-start | bytes 3145728 | tf_op jit(solution)/shard_map/reduce_scatter | solution.py:103
  166.9 1.9 copy-start
  168.8 6.5 %copy-start.7 = (f32[256,16]{0,1:T(8,128)S(1)}, f32[256,16]{0,1:T(8,128)}, u32[]{:S(2)}) copy-start(f32[256,16]{0,1:T(8,128)} %param.21) | copy-start | bytes 49156
  168.8 6.5 %copy-start.9 = (f32[256]{0:T(256)S(1)}, f32[256]{0:T(256)}, u32[]{:S(2)}) copy-start(f32[256]{0:T(256)} %param.20) | copy-start | bytes 3076
  201.9 10.2 %copy-start.10 = (bf16[2048,1024]{1,0:T(8,128)(2,1)S(1)}, bf16[2048,1024]{1,0:T(8,128)(2,1)}, u32[]{:S(2)}) copy-start(bf16[2048,1024]{1,0:T(8,128)(2,1)} %param.18) | copy-start | bytes 12582916
  214.8 106.2 %reduce-scatter.5.cloned.1.call-start = ((), (), s32[]{:S(2)}) async-start(), calls=%async_computation.6 | async-start | bytes 4456448 | tf_op jit(solution)/shard_map/reduce_scatter | solution.py:106
  247.9 116.3 %copy-start.5 = (f32[256,16]{0,1:T(8,128)S(1)}, f32[256,16]{0,1:T(8,128)}, u32[]{:S(2)}) copy-start(f32[256,16]{0,1:T(8,128)} %param.26) | copy-start | bytes 49156
  247.9 116.3 %copy-start.6 = (f32[256,16]{0,1:T(8,128)S(1)}, f32[256,16]{0,1:T(8,128)}, u32[]{:S(2)}) copy-start(f32[256,16]{0,1:T(8,128)} %param.27) | copy-start | bytes 49156
  247.9 117.0 %copy-start.1 = (f32[64,1024]{1,0:T(8,128)S(1)}, f32[64,1024]{1,0:T(8,128)}, u32[]{:S(2)}) copy-start(f32[64,1024]{1,0:T(8,128)} %param.22) | copy-start | bytes 786436
  247.9 117.0 %copy-start.2 = (f32[64,1024]{1,0:T(8,128)S(1)}, f32[64,1024]{1,0:T(8,128)}, u32[]{:S(2)}) copy-start(f32[64,1024]{1,0:T(8,128)} %param.23) | copy-start | bytes 786436
  247.9 117.0 %copy-start.3 = (f32[64,1024]{1,0:T(8,128)S(1)}, f32[64,1024]{1,0:T(8,128)}, u32[]{:S(2)}) copy-start(f32[64,1024]{1,0:T(8,128)} %param.24) | copy-start | bytes 786436
Sparse Core Ops, SparseCore 0:
  10.7 44.1 all-gather.4
  58.2 19.9 all-gather.6
  85.7 75.1 all-gather.8
  214.9 29.0 reduce-scatter.2
  248.1 72.8 reduce-scatter.4
